TPU v7x, 256 devices: a whole 4x4x8 slice. The times are simulated.
256 devices in a mesh: seq: 32 (over x, z_hi, core), tensor: 8 (over z_lo, y).
Axes of the slice: x: 4, y: 4, z: 8 (z_hi: 4, z_lo: 2; z = z_hi * 2 + z_lo), core: 2. Of those that a mesh axis runs over, the one named last changes fastest.
Arguments:
- keyval: bfloat16 [16384, 8192], P('seq', 'tensor'), may hold values from -6 to 6
- gating: bfloat16 [16384, 8192], P('seq', 'tensor'), may hold values from -6 to 6
- skip_gain: float32 [8192], P('tensor'), may hold values from -4 to 4
- filter_values: float32 [2, 64, 2, 32, 8192], P(None, None, None, 'seq', 'tensor'), may hold values from -12 to 12
- blocks: int32 [64, 64], P('tensor'), may hold values from 0 to 255, as said below
- out_weight: bfloat16 [8192, 8192], P('seq', 'tensor'), may hold values from -0.0625 to 0.0625
Outputs:
- mixed: bfloat16 [16384, 8192], P('seq', 'tensor')
Inputs may be any that keep to these rules, and one draw needn't show every extreme that they name: Each row names 64 different blocks.
All inputs are finite; a program needn't handle non-finite values.
Results may differ from a plain program's by a relative error of at most 0.0063.
Values may be sent and summed in bfloat16 or wider, within the bound.
A program may use at most 128 MiB of HBM per device.

v0:
```python
import math
import jax
import jax.numpy as jnp
from jax import lax
from jax.sharding import PartitionSpec as P

BLOCK = 64
HIGHEST = lax.Precision.HIGHEST


def tables(first_index, second_index, length):
    phase = first_index * second_index % length
    angle = 2.0 * math.pi / length * phase.astype(jnp.float32)
    return (jnp.cos(angle), jnp.sin(angle))


def rounded(value):
    return lax.optimization_barrier(value.astype(jnp.bfloat16)).astype(jnp.float32)


def whole_conv(signal_group, block_list, filter_group, cycle_size, tokens_local):
    seq_length = cycle_size * tokens_local
    unit = signal_group.shape[1]
    repeat = filter_group.shape[2]
    signal = signal_group.astype(jnp.float32).reshape(cycle_size, tokens_local, unit)
    cycle_index = jnp.arange(cycle_size, dtype=jnp.int32)
    local_index = jnp.arange(tokens_local, dtype=jnp.int32)
    cosine_cycle, sine_cycle = tables(cycle_index[:, None], cycle_index[None, :], cycle_size)
    first_real = jnp.einsum("pa,ajc->pjc", cosine_cycle, signal, precision=HIGHEST)
    first_imaginary = -jnp.einsum("pa,ajc->pjc", sine_cycle, signal, precision=HIGHEST)
    cosine_twist, sine_twist = tables(cycle_index[:, None], local_index[None, :], seq_length)
    cosine_twist = cosine_twist[:, :, None]
    sine_twist = sine_twist[:, :, None]
    twist_real = rounded(first_real * cosine_twist + first_imaginary * sine_twist)
    twist_imaginary = rounded(first_imaginary * cosine_twist - first_real * sine_twist)
    kept_rows = (
        block_list[:, None] * repeat + jnp.arange(repeat, dtype=jnp.int32)[None, :]
    ).reshape(-1)
    cosine_kept, sine_kept = tables(kept_rows[:, None], local_index[None, :], tokens_local)
    spectrum_real = jnp.einsum(
        "qj,pjc->pqc", cosine_kept, twist_real, precision=HIGHEST
    ) + jnp.einsum("qj,pjc->pqc", sine_kept, twist_imaginary, precision=HIGHEST)
    spectrum_imaginary = jnp.einsum(
        "qj,pjc->pqc", cosine_kept, twist_imaginary, precision=HIGHEST
    ) - jnp.einsum("qj,pjc->pqc", sine_kept, twist_real, precision=HIGHEST)
    filter_real = filter_group[0].reshape(-1, cycle_size, unit).transpose(1, 0, 2)
    filter_imaginary = filter_group[1].reshape(-1, cycle_size, unit).transpose(1, 0, 2)
    product_real = filter_real * spectrum_real - filter_imaginary * spectrum_imaginary
    product_imaginary = filter_real * spectrum_imaginary + filter_imaginary * spectrum_real
    back_real = jnp.einsum(
        "qj,pqc->pjc", cosine_kept, product_real, precision=HIGHEST
    ) - jnp.einsum("qj,pqc->pjc", sine_kept, product_imaginary, precision=HIGHEST)
    back_imaginary = jnp.einsum(
        "qj,pqc->pjc", sine_kept, product_real, precision=HIGHEST
    ) + jnp.einsum("qj,pqc->pjc", cosine_kept, product_imaginary, precision=HIGHEST)
    turned_real = rounded(back_real * cosine_twist - back_imaginary * sine_twist)
    turned_imaginary = rounded(back_real * sine_twist + back_imaginary * cosine_twist)
    convolved = (
        jnp.einsum("pa,pjc->ajc", cosine_cycle, turned_real, precision=HIGHEST)
        - jnp.einsum("pa,pjc->ajc", sine_cycle, turned_imaginary, precision=HIGHEST)
    ) / seq_length
    return convolved.astype(jnp.bfloat16).reshape(seq_length, unit)


def body(keyval, gating, skip_gain, filter_values, blocks, out_weight):
    cycle_size = lax.axis_size("seq")
    cycle_pos = lax.axis_index("seq")
    tokens_local, channels = keyval.shape
    seq_length = tokens_local * cycle_size
    repeat = BLOCK // cycle_size
    groups_local = blocks.shape[0]
    group_width = channels // groups_local
    whole_weight = lax.all_gather(out_weight, "seq", axis=0, tiled=True)
    narrow = channels // cycle_size
    unit = min(narrow, group_width)
    subgroups = narrow // unit
    columns = lax.all_to_all(keyval, "seq", split_axis=1, concat_axis=0, tiled=True)
    filter_cols = lax.all_to_all(filter_values, "seq", split_axis=4, concat_axis=3, tiled=True)
    sub_group = (cycle_pos * narrow + jnp.arange(subgroups, dtype=jnp.int32) * unit) // group_width
    match = sub_group[:, None, None] == jnp.arange(groups_local, dtype=jnp.int32)[None, :, None]
    sub_blocks = jnp.sum(jnp.where(match, blocks[None, :, :], 0), axis=1)
    sub_signal = columns.reshape(seq_length, subgroups, unit).transpose(1, 0, 2)
    sub_filters = filter_cols.reshape(
        2, filter_cols.shape[1], repeat, cycle_size, subgroups, unit
    ).transpose(4, 0, 1, 2, 3, 5)

    def sub_step(items):
        return whole_conv(items[0], items[1], items[2], cycle_size, tokens_local)

    done = lax.map(sub_step, (sub_signal, sub_blocks, sub_filters))
    done = done.transpose(1, 0, 2).reshape(seq_length, narrow)
    convolved = lax.all_to_all(done, "seq", split_axis=0, concat_axis=1, tiled=True)
    hidden = (
        gating.astype(jnp.float32)
        * (convolved.astype(jnp.float32) + skip_gain[None, :] * keyval.astype(jnp.float32))
    ).astype(jnp.bfloat16)
    full_hidden = lax.all_gather(hidden, "tensor", axis=1, tiled=True)
    mixed_rows = jnp.dot(full_hidden, whole_weight, preferred_element_type=jnp.float32)
    return mixed_rows.astype(jnp.bfloat16)


def solution(mesh):
    placed = (
        P("seq", "tensor"),
        P("seq", "tensor"),
        P("tensor"),
        P(None, None, None, "seq", "tensor"),
        P("tensor", None),
        P("seq", "tensor"),
    )
    return jax.shard_map(
        body, mesh=mesh, in_specs=placed, out_specs=P("seq", "tensor"), check_vma=False
    )
```

profile of v0, /device:TPU:33, one launch (start us, length us, event | category | flops | bytes accessed | tf_op | source)
XLA Modules:
  0.0 406.2 jit_solution(17398672774952115893)
XLA Ops:
  6.5 2.3 copy.54
  8.8 10.9 %all-to-all-start.1 = ((bf16[512,32,32]{0,2,1:T(8,128)(2,1)}), bf16[512,32,32]{0,2,1:T(8,128)(2,1)S(1)}, u32[]{:S(2)}, u32[]{:S(2)}) async-start(bf16[512,32,32]{0,2,1:T(8,128)(2,1)} %bitcast.3), calls=%async_computation.1 | async-start | bytes 2097152 | tf_op jit(solution)/shard_map/all_to_all | solution.py:77
  19.7 4.2 %copy.51 = f32[2,64,2,1,1024]{1,2,3,0,4:T(2,128)S(1)} copy(f32[2,64,2,1,1024]{4,3,2,1,0:T(1,128)} %param.9) | data formatting | bytes 2097152 | tf_op args[3]
  23.9 3.2 reshape.112
  27.2 21.8 %all-to-all-done.1 = bf16[512,32,32]{0,2,1:T(8,128)(2,1)S(1)} async-done(((bf16[512,32,32]{0,2,1:T(8,128)(2,1)}), bf16[512,32,32]{0,2,1:T(8,128)(2,1)S(1)}, u32[]{:S(2)}, u32[]{:S(2)}) %all-to-all-start.1) | async-done | bytes 1048608 | tf_op jit(solution)/shard_map/all_to_all | solution.py:77
  49.0 4.8 %all-to-all-start = ((f32[32,1,8192]{2,1,0:T(1,128)}), f32[32,1,8192]{2,1,0:T(1,128)S(1)}, u32[]{:S(2)}, u32[]{:S(2)}) async-start(f32[32,1,8192]{2,1,0:T(1,128)} %reshape.112), calls=%async_computation | async-start | bytes 2097152 | tf_op jit(solution)/shard_map/all_to_all | solution.py:78
  57.9 2.5 fusion.13
  60.3 3.3 fusion.17
  63.6 3.3 fusion.2
  66.9 16.2 %all-to-all-done = f32[32,1,8192]{2,1,0:T(1,128)S(1)} async-done(((f32[32,1,8192]{2,1,0:T(1,128)}), f32[32,1,8192]{2,1,0:T(1,128)S(1)}, u32[]{:S(2)}, u32[]{:S(2)}) %all-to-all-start) | async-done | bytes 1048608 | tf_op jit(solution)/shard_map/all_to_all | solution.py:78
  83.6 16.2 %reduce.2 = f32[32,8192]{1,0:T(8,128)S(1)} reduce(f32[32,1,8192]{2,1,0:T(1,128)S(1)} %all-to-all-done, f32[]{:T(128)} %broadcast.243), dimensions={1}, to_apply=%all_to_all.12.reduce_sub_computation | reduce | bytes 2097156 | tf_op jit(solution)/shard_map/all_to_all | solution.py:78
  103.0 2.1 copy.52
  112.4 2.1 copy.61
  114.5 4.0 fusion.22
  118.5 2.8 fusion.26
  121.3 2.8 fusion.32
  124.1 2.8 convolution_add_fusion
  126.9 3.7 fusion.5
  135.3 4.1 %all-to-all-start.2 = ((bf16[32,512,32]{1,2,0:T(8,128)(2,1)}), bf16[32,512,32]{1,2,0:T(8,128)(2,1)S(1)}, u32[]{:S(2)}, u32[]{:S(2)}) async-start(bf16[32,512,32]{1,2,0:T(8,128)(2,1)} %copy.66), calls=%async_computation.2 | async-start | bytes 2097152 | tf_op jit(solution)/shard_map/all_to_all | solution.py:92
  140.1 29.2 %all-to-all-done.2 = bf16[32,512,32]{1,2,0:T(8,128)(2,1)S(1)} async-done(((bf16[32,512,32]{1,2,0:T(8,128)(2,1)}), bf16[32,512,32]{1,2,0:T(8,128)(2,1)S(1)}, u32[]{:S(2)}, u32[]{:S(2)}) %all-to-all-start.2) | async-done | bytes 1048608 | tf_op jit(solution)/shard_map/all_to_all | solution.py:92
  169.3 2.7 fusion.1
  172.8 88.6 %all-gather.3.cloned.1.call-done = bf16[512,8192]{0,1:T(8,128)(2,1)} async-done(((bf16[512,1024]{0,1:T(8,128)(2,1)}), bf16[512,8192]{0,1:T(8,128)(2,1)}) %all-gather.3.cloned.1.call-update) | async-done | bytes 8388624 | tf_op jit(solution)/shard_map/all_gather | solution.py:97
  261.4 122.2 %all-gather.5.cloned.1.call-done = bf16[8192,1024]{1,0:T(8,128)(2,1)} async-done(((bf16[256,1024]{1,0:T(8,128)(2,1)}), bf16[8192,1024]{1,0:T(8,128)(2,1)}) %all-gather.5.cloned.1.call-update) | async-done | bytes 16777232 | tf_op jit(solution)/shard_map/all_gather | solution.py:73
  383.5 15.6 %convolution_convert_fusion = bf16[512,1024]{1,0:T(8,128)(2,1)} fusion(bf16[512,8192]{0,1:T(8,128)(2,1)} %all-gather.3.cloned.1.call-done, bf16[8192,1024]{1,0:T(8,128)(2,1)} %all-gather.5.cloned.1.call-done), kind=kOutput, calls=%fused_computation.10 | convolution fusion | flops 8590458880 | bytes 26214400 | tf_op jit(solution)/shard_map/dot_general | solution.py:98
  (33 shorter events, 21.1 us)
Async XLA Ops:
  8.8 40.2 %all-to-all-start.1 = ((bf16[512,32,32]{0,2,1:T(8,128)(2,1)}), bf16[512,32,32]{0,2,1:T(8,128)(2,1)S(1)}, u32[]{:S(2)}, u32[]{:S(2)}) async-start(bf16[512,32,32]{0,2,1:T(8,128)(2,1)} %bitcast.3), calls=%async_computation.1 | async-start | bytes 2097152 | tf_op jit(solution)/shard_map/all_to_all | solution.py:77
  23.9 3.2 copy-start.4
  49.0 34.1 %all-to-all-start = ((f32[32,1,8192]{2,1,0:T(1,128)}), f32[32,1,8192]{2,1,0:T(1,128)S(1)}, u32[]{:S(2)}, u32[]{:S(2)}) async-start(f32[32,1,8192]{2,1,0:T(1,128)} %reshape.112), calls=%async_computation | async-start | bytes 2097152 | tf_op jit(solution)/shard_map/all_to_all | solution.py:78
  57.8 5.8 %copy-start = (bf16[32,512,32]{1,0,2:T(8,128)(2,1)}, bf16[32,512,32]{1,0,2:T(8,128)(2,1)S(1)}, u32[]{:S(2)}) copy-start(bf16[32,512,32]{1,0,2:T(8,128)(2,1)S(1)} %get-tuple-element.22) | copy-start | bytes 3145732
  110.4 4.1 %copy-start.1 = (bf16[32,512,32]{1,0,2:T(8,128)(2,1)S(1)}, bf16[32,512,32]{1,0,2:T(8,128)(2,1)}, u32[]{:S(2)}) copy-start(bf16[32,512,32]{1,0,2:T(8,128)(2,1)} %copy-done) | copy-start | bytes 3145732
  133.8 5.8 %copy-start.2 = (bf16[512,1024]{1,0:T(8,128)(2,1)S(1)}, bf16[512,1024]{1,0:T(8,128)(2,1)}, u32[]{:S(2)}) copy-start(bf16[512,1024]{1,0:T(8,128)(2,1)} %param.7) | copy-start | bytes 3145732
  135.3 34.0 %copy-start.3 = (f32[1024]{0:T(1024)S(1)}, f32[1024]{0:T(1024)}, u32[]{:S(2)}) copy-start(f32[1024]{0:T(1024)} %param.8) | copy-start | bytes 12292
  135.3 34.0 %all-to-all-start.2 = ((bf16[32,512,32]{1,2,0:T(8,128)(2,1)}), bf16[32,512,32]{1,2,0:T(8,128)(2,1)S(1)}, u32[]{:S(2)}, u32[]{:S(2)}) async-start(bf16[32,512,32]{1,2,0:T(8,128)(2,1)} %copy.66), calls=%async_computation.2 | async-start | bytes 2097152 | tf_op jit(solution)/shard_map/all_to_all | solution.py:92
  139.5 121.9 %all-gather.3.cloned.1.call-start = ((), (), s32[]{:S(2)}) async-start(), calls=%async_computation.3 | async-start | bytes 9437184 | tf_op jit(solution)/shard_map/all_gather | solution.py:97
  172.0 211.5 %all-gather.5.cloned.1.call-start = ((), (), s32[]{:S(2)}) async-start(), calls=%async_computation.4 | async-start | bytes 17301504 | tf_op jit(solution)/shard_map/all_gather | solution.py:73
Sparse Core Ops, SparseCore 0:
  172.2 89.1 all-gather.2
  263.9 119.5 all-gather.4
where the time goes:
time: 410 us; the launch traced here: 406 us
  waiting for transfers between devices  279 us (68%)
  matrix products  47.4 us (12%)
  local copies, waits for them, and re-layouts  27.1 us (7%)
  starting transfers between devices  19.8 us (5%)
  other arithmetic  19.3 us (5%)
  between operations  13.8 us (3%)
    all_gather x1, waiting for transfers between devices, body(): whole_weight = lax.all_gather(out_weight, 'seq', axis=0, tiled=True)  122 us
    all_gather x1, waiting for transfers between devices, body(): full_hidden = lax.all_gather(hidden, 'tensor', axis=1, tiled=True)  88.6 us
    all_to_all x1, waiting for transfers between devices, body(): lax.all_to_all(done, 'seq', split_axis=0, concat_axis=1, tiled=True)  29.2 us
    all_to_all x1, waiting for transfers between devices, body(): lax.all_to_all(keyval, 'seq', split_axis=1, concat_axis=0, tiled=True)  21.8 us
    all_to_all x1, other arithmetic, body(): lax.all_to_all(filter_values, 'seq', split_axis=4, concat_axis=3, tiled=T...  16.2 us
    all_to_all x1, waiting for transfers between devices, body(): lax.all_to_all(filter_values, 'seq', split_axis=4, concat_axis=3, tiled=T...  16.2 us
    dot_general x1, matrix products, body(): jnp.dot(full_hidden, whole_weight, preferred_element_type=jnp.float32)  15.6 us
    unnamed x15, local copies, waits for them, and re-layouts  11.7 us
  transfers between devices with their start and end apart: 5, of which 5 were waited for; matrix products, arithmetic and copies ran while one was open for 5% of the time, Pallas kernels for 0%

commit v1 on v0

--- a/solution.py
+++ b/solution.py
@@ -89,7 +89,10 @@
 
     done = lax.map(sub_step, (sub_signal, sub_blocks, sub_filters))
     done = done.transpose(1, 0, 2).reshape(seq_length, narrow)
-    convolved = lax.all_to_all(done, "seq", split_axis=0, concat_axis=1, tiled=True)
+    convolved = jnp.concatenate(
+        lax.all_to_all(jnp.stack(jnp.split(done, lax.axis_size("seq"), axis=0)), "seq", 0, 0),
+        axis=1,
+    )
     hidden = (
         gating.astype(jnp.float32)
         * (convolved.astype(jnp.float32) + skip_gain[None, :] * keyval.astype(jnp.float32))

time: 410 us -> 410 us (level)
  no operation moved by 1% of the time
where the time goes in v1:
time: 410 us; the launch traced here: 406 us
  waiting for transfers between devices  279 us (68%)
  matrix products  47.4 us (12%)
  local copies, waits for them, and re-layouts  27.1 us (7%)
  starting transfers between devices  19.8 us (5%)
  other arithmetic  19.3 us (5%)
  between operations  13.8 us (3%)
    all_gather x1, waiting for transfers between devices, body(): whole_weight = lax.all_gather(out_weight, 'seq', axis=0, tiled=True)  122 us
    all_gather x1, waiting for transfers between devices, body(): full_hidden = lax.all_gather(hidden, 'tensor', axis=1, tiled=True)  88.6 us
    all_to_all x1, waiting for transfers between devices, body(): lax.all_to_all(jnp.stack(jnp.split(done, lax.axis_size('seq'), axis=0)),...  29.2 us
    all_to_all x1, waiting for transfers between devices, body(): lax.all_to_all(keyval, 'seq', split_axis=1, concat_axis=0, tiled=True)  21.8 us
    all_to_all x1, other arithmetic, body(): lax.all_to_all(filter_values, 'seq', split_axis=4, concat_axis=3, tiled=T...  16.2 us
    all_to_all x1, waiting for transfers between devices, body(): lax.all_to_all(filter_values, 'seq', split_axis=4, concat_axis=3, tiled=T...  16.2 us
    dot_general x1, matrix products, body(): jnp.dot(full_hidden, whole_weight, preferred_element_type=jnp.float32)  15.6 us
    unnamed x15, local copies, waits for them, and re-layouts  11.7 us
  transfers between devices with their start and end apart: 5, of which 5 were waited for; matrix products, arithmetic and copies ran while one was open for 5% of the time, Pallas kernels for 0%

profile of v1, /device:TPU:33, one launch (start us, length us, event | category | flops | bytes accessed | tf_op | source)
XLA Modules:
  0.0 406.2 jit_solution(17398672774952115893)
XLA Ops:
  6.5 2.3 copy.54
  8.8 10.9 %all-to-all-start.1 = ((bf16[512,32,32]{0,2,1:T(8,128)(2,1)}), bf16[512,32,32]{0,2,1:T(8,128)(2,1)S(1)}, u32[]{:S(2)}, u32[]{:S(2)}) async-start(bf16[512,32,32]{0,2,1:T(8,128)(2,1)} %bitcast.3), calls=%async_computation.1 | async-start | bytes 2097152 | tf_op jit(solution)/shard_map/all_to_all | solution.py:77
  19.7 4.2 %copy.51 = f32[2,64,2,1,1024]{1,2,3,0,4:T(2,128)S(1)} copy(f32[2,64,2,1,1024]{4,3,2,1,0:T(1,128)} %param.9) | data formatting | bytes 2097152 | tf_op args[3]
  23.9 3.2 reshape.174
  27.2 21.8 %all-to-all-done.1 = bf16[512,32,32]{0,2,1:T(8,128)(2,1)S(1)} async-done(((bf16[512,32,32]{0,2,1:T(8,128)(2,1)}), bf16[512,32,32]{0,2,1:T(8,128)(2,1)S(1)}, u32[]{:S(2)}, u32[]{:S(2)}) %all-to-all-start.1) | async-done | bytes 1048608 | tf_op jit(solution)/shard_map/all_to_all | solution.py:77
  49.0 4.8 %all-to-all-start = ((f32[32,1,8192]{2,1,0:T(1,128)}), f32[32,1,8192]{2,1,0:T(1,128)S(1)}, u32[]{:S(2)}, u32[]{:S(2)}) async-start(f32[32,1,8192]{2,1,0:T(1,128)} %reshape.174), calls=%async_computation | async-start | bytes 2097152 | tf_op jit(solution)/shard_map/all_to_all | solution.py:78
  57.9 2.5 fusion.13
  60.3 3.3 fusion.17
  63.6 3.3 fusion.2
  66.9 16.2 %all-to-all-done = f32[32,1,8192]{2,1,0:T(1,128)S(1)} async-done(((f32[32,1,8192]{2,1,0:T(1,128)}), f32[32,1,8192]{2,1,0:T(1,128)S(1)}, u32[]{:S(2)}, u32[]{:S(2)}) %all-to-all-start) | async-done | bytes 1048608 | tf_op jit(solution)/shard_map/all_to_all | solution.py:78
  83.6 16.2 %reduce.2 = f32[32,8192]{1,0:T(8,128)S(1)} reduce(f32[32,1,8192]{2,1,0:T(1,128)S(1)} %all-to-all-done, f32[]{:T(128)} %broadcast.243), dimensions={1}, to_apply=%all_to_all.22.reduce_sub_computation | reduce | bytes 2097156 | tf_op jit(solution)/shard_map/all_to_all | solution.py:78
  103.0 2.1 copy.52
  112.4 2.1 copy.61
  114.5 4.0 fusion.22
  118.5 2.8 fusion.26
  121.3 2.8 fusion.32
  124.1 2.8 convolution_add_fusion
  126.9 3.7 fusion.5
  135.3 4.1 %all-to-all-start.2 = ((bf16[32,512,32]{1,2,0:T(8,128)(2,1)}), bf16[32,512,32]{1,2,0:T(8,128)(2,1)S(1)}, u32[]{:S(2)}, u32[]{:S(2)}) async-start(bf16[32,512,32]{1,2,0:T(8,128)(2,1)} %copy.66), calls=%async_computation.2 | async-start | bytes 2097152 | tf_op jit(solution)/shard_map/all_to_all | solution.py:93
  140.1 29.2 %all-to-all-done.2 = bf16[32,512,32]{1,2,0:T(8,128)(2,1)S(1)} async-done(((bf16[32,512,32]{1,2,0:T(8,128)(2,1)}), bf16[32,512,32]{1,2,0:T(8,128)(2,1)S(1)}, u32[]{:S(2)}, u32[]{:S(2)}) %all-to-all-start.2) | async-done | bytes 1048608 | tf_op jit(solution)/shard_map/all_to_all | solution.py:93
  169.3 2.7 fusion.1
  172.8 88.6 %all-gather.3.cloned.1.call-done = bf16[512,8192]{0,1:T(8,128)(2,1)} async-done(((bf16[512,1024]{0,1:T(8,128)(2,1)}), bf16[512,8192]{0,1:T(8,128)(2,1)}) %all-gather.3.cloned.1.call-update) | async-done | bytes 8388624 | tf_op jit(solution)/shard_map/all_gather | solution.py:100
  261.4 122.2 %all-gather.5.cloned.1.call-done = bf16[8192,1024]{1,0:T(8,128)(2,1)} async-done(((bf16[256,1024]{1,0:T(8,128)(2,1)}), bf16[8192,1024]{1,0:T(8,128)(2,1)}) %all-gather.5.cloned.1.call-update) | async-done | bytes 16777232 | tf_op jit(solution)/shard_map/all_gather | solution.py:73
  383.5 15.6 %convolution_convert_fusion = bf16[512,1024]{1,0:T(8,128)(2,1)} fusion(bf16[512,8192]{0,1:T(8,128)(2,1)} %all-gather.3.cloned.1.call-done, bf16[8192,1024]{1,0:T(8,128)(2,1)} %all-gather.5.cloned.1.call-done), kind=kOutput, calls=%fused_computation.10 | convolution fusion | flops 8590458880 | bytes 26214400 | tf_op jit(solution)/shard_map/dot_general | solution.py:101
  (33 shorter events, 21.1 us)
Async XLA Ops:
  8.8 40.2 %all-to-all-start.1 = ((bf16[512,32,32]{0,2,1:T(8,128)(2,1)}), bf16[512,32,32]{0,2,1:T(8,128)(2,1)S(1)}, u32[]{:S(2)}, u32[]{:S(2)}) async-start(bf16[512,32,32]{0,2,1:T(8,128)(2,1)} %bitcast.3), calls=%async_computation.1 | async-start | bytes 2097152 | tf_op jit(solution)/shard_map/all_to_all | solution.py:77
  23.9 3.2 copy-start.4
  49.0 34.1 %all-to-all-start = ((f32[32,1,8192]{2,1,0:T(1,128)}), f32[32,1,8192]{2,1,0:T(1,128)S(1)}, u32[]{:S(2)}, u32[]{:S(2)}) async-start(f32[32,1,8192]{2,1,0:T(1,128)} %reshape.174), calls=%async_computation | async-start | bytes 2097152 | tf_op jit(solution)/shard_map/all_to_all | solution.py:78
  57.8 5.8 %copy-start = (bf16[32,512,32]{1,0,2:T(8,128)(2,1)}, bf16[32,512,32]{1,0,2:T(8,128)(2,1)S(1)}, u32[]{:S(2)}) copy-start(bf16[32,512,32]{1,0,2:T(8,128)(2,1)S(1)} %get-tuple-element.22) | copy-start | bytes 3145732
  110.4 4.1 %copy-start.1 = (bf16[32,512,32]{1,0,2:T(8,128)(2,1)S(1)}, bf16[32,512,32]{1,0,2:T(8,128)(2,1)}, u32[]{:S(2)}) copy-start(bf16[32,512,32]{1,0,2:T(8,128)(2,1)} %copy-done) | copy-start | bytes 3145732
  133.8 5.8 %copy-start.2 = (bf16[512,1024]{1,0:T(8,128)(2,1)S(1)}, bf16[512,1024]{1,0:T(8,128)(2,1)}, u32[]{:S(2)}) copy-start(bf16[512,1024]{1,0:T(8,128)(2,1)} %param.7) | copy-start | bytes 3145732
  135.3 34.0 %copy-start.3 = (f32[1024]{0:T(1024)S(1)}, f32[1024]{0:T(1024)}, u32[]{:S(2)}) copy-start(f32[1024]{0:T(1024)} %param.8) | copy-start | bytes 12292
  135.3 34.0 %all-to-all-start.2 = ((bf16[32,512,32]{1,2,0:T(8,128)(2,1)}), bf16[32,512,32]{1,2,0:T(8,128)(2,1)S(1)}, u32[]{:S(2)}, u32[]{:S(2)}) async-start(bf16[32,512,32]{1,2,0:T(8,128)(2,1)} %copy.66), calls=%async_computation.2 | async-start | bytes 2097152 | tf_op jit(solution)/shard_map/all_to_all | solution.py:93
  139.5 121.9 %all-gather.3.cloned.1.call-start = ((), (), s32[]{:S(2)}) async-start(), calls=%async_computation.3 | async-start | bytes 9437184 | tf_op jit(solution)/shard_map/all_gather | solution.py:100
  172.0 211.5 %all-gather.5.cloned.1.call-start = ((), (), s32[]{:S(2)}) async-start(), calls=%async_computation.4 | async-start | bytes 17301504 | tf_op jit(solution)/shard_map/all_gather | solution.py:73
Sparse Core Ops, SparseCore 0:
  172.2 89.1 all-gather.2
  263.9 119.5 all-gather.4
